TPU v7x, 32 devices: a whole 2x2x4 slice. The times are simulated.
32 devices in a mesh: seq: 2 (over x), tensor: 16 (over z, y, core).
Axes of the slice: x: 2, y: 2, z: 4, core: 2. Of those that a mesh axis runs over, the one named last changes fastest.
Arguments:
- tokens: bfloat16 [512, 4096], P(('seq', 'tensor')), may hold values from -6 to 6
- lengths: int32 [6], replicated, may hold values from 1 to 256, 512 in all
- proj_zx: bfloat16 [4096, 2, 8192], P(None, None, 'tensor'), may hold values from -0.09375 to 0.09375
- proj_bc: bfloat16 [4096, 2, 1024], P(None, None, 'tensor'), may hold values from -0.09375 to 0.09375
- proj_dt: bfloat16 [4096, 128], P(None, 'tensor'), may hold values from -0.09375 to 0.09375
- conv_x: float32 [4, 8192], P(None, 'tensor'), may hold values from -3 to 3
- conv_bc: float32 [4, 2, 1024], P(None, None, 'tensor'), may hold values from -3 to 3
- bias_x: float32 [8192], P('tensor'), may hold values from -0.5 to 0.5
- bias_bc: float32 [2, 1024], P(None, 'tensor'), may hold values from -0.5 to 0.5
- dt_bias: float32 [128], P('tensor'), may hold values from -7 to -3
- decay_rate: float32 [128], P('tensor'), may hold values from 0.02 to 1
- skip_gain: float32 [128], P('tensor'), may hold values from 0.5 to 1.5
- proj_out: bfloat16 [8192, 4096], P('tensor'), may hold values from -0.0625 to 0.0625
Outputs:
- mixed: bfloat16 [512, 4096], P(('seq', 'tensor'))
- final_states: float32 [6, 128, 64, 128], P(None, 'tensor')
Inputs may be any that keep to these rules, and one draw needn't show every extreme that they name: `lengths`: the 6 requests lie back to back in the stream in this order and fill it exactly; the longest has exactly 256 tokens.
All inputs are finite; a program needn't handle non-finite values.
Results may differ from a plain program's by a relative error of at most 0.0074.
Values may be sent and summed in bfloat16 or wider, within the bound.
A program may use at most 128 MiB of HBM per device.

v0:
```python
import jax
import jax.numpy as jnp
from jax import lax
from jax.sharding import PartitionSpec as P

GROUPS = 8


def partner_2(value, axis, bit):
    mask = 2**bit
    pairs = [(source, source ^ mask) for source in range(lax.axis_size(axis))]
    return lax.ppermute(value, axis, pairs)


def passed_along(block, axis, distance):
    devices = range(lax.axis_size(axis))
    route = [(i - distance, i) for i in devices if i - distance in devices]
    return lax.ppermute(block, axis, route)


def group_columns(bc_own, tensor_index, steps_count):
    collected = bc_own
    for bit_number in range(steps_count):
        partner = partner_2(collected, "tensor", bit_number)
        upper = tensor_index // 2**bit_number % 2
        low_first = jnp.concatenate([collected, partner], axis=2)
        high_first = jnp.concatenate([partner, collected], axis=2)
        collected = jnp.where(upper == 0, low_first, high_first)
    return collected


def body(
    tokens,
    lengths,
    proj_zx,
    proj_bc,
    proj_dt,
    conv_x,
    conv_bc,
    bias_x,
    bias_bc,
    dt_bias,
    decay_rate,
    skip_gain,
    proj_out,
):
    highest = lax.Precision.HIGHEST
    tensor_size = lax.axis_size("tensor")
    rows_dev = tokens.shape[0]
    shard_len = rows_dev * tensor_size
    seq_index = lax.axis_index("seq")
    tensor_index = lax.axis_index("tensor")
    heads_dev = decay_rate.shape[0]
    width_zx = proj_zx.shape[2]
    head_size = width_zx // heads_dev
    cols_bc = proj_bc.shape[2]
    taps_count = conv_x.shape[0]
    model_width = tokens.shape[1]
    zx_flat = proj_zx.reshape(model_width, 2 * width_zx)
    bc_flat = proj_bc.reshape(model_width, 2 * cols_bc)
    piece = lax.all_gather(tokens, "tensor", axis=0, tiled=True)
    projected = jnp.concatenate(
        [
            jnp.dot(piece, zx_flat, preferred_element_type=jnp.float32),
            jnp.dot(piece, bc_flat, preferred_element_type=jnp.float32),
            jnp.dot(piece, proj_dt, preferred_element_type=jnp.float32),
        ],
        axis=1,
    )
    gate_in = projected[:, :width_zx].astype(jnp.bfloat16)
    conv_in = projected[:, width_zx : 2 * width_zx + 2 * cols_bc].astype(jnp.bfloat16)
    step_size = jax.nn.softplus(projected[:, 2 * width_zx + 2 * cols_bc :] + dt_bias[None, :])
    row_ids = jnp.arange(shard_len, dtype=jnp.int32)
    positions = seq_index * shard_len + row_ids
    bounds = jnp.cumsum(lengths)
    reached = bounds[None, :] <= positions[:, None]
    segment = jnp.sum(reached.astype(jnp.int32), axis=1)
    seg_start = jnp.max(jnp.where(reached, bounds[None, :], 0), axis=1)
    edge_rows = conv_in[shard_len - (taps_count - 1) :]
    before = passed_along(edge_rows, "seq", 1)
    extended = jnp.concatenate([before, conv_in], axis=0)
    conv_taps = jnp.concatenate([conv_x, conv_bc.reshape(taps_count, 2 * cols_bc)], axis=1)
    conv_offset = jnp.concatenate([bias_x, bias_bc.reshape(2 * cols_bc)])
    convolved = jnp.zeros((shard_len, conv_taps.shape[1]), jnp.float32) + conv_offset[None, :]
    for lag_index in range(taps_count):
        lagged = extended[
            taps_count - 1 - lag_index : taps_count - 1 - lag_index + shard_len
        ].astype(jnp.float32)
        keep_mask = (positions - lag_index >= seg_start).astype(jnp.float32)
        convolved = convolved + conv_taps[lag_index][None, :] * lagged * keep_mask[:, None]
    activated = jax.nn.silu(convolved).astype(jnp.bfloat16)
    x_conv = activated[:, :width_zx]
    bc_own = activated[:, width_zx:].reshape(shard_len, 2, cols_bc)
    per_group = tensor_size // GROUPS
    steps_count = per_group.bit_length() - 1
    bc_group = group_columns(bc_own, tensor_index, steps_count).astype(jnp.float32)
    state_in_proj = bc_group[:, 0]
    state_out_proj = bc_group[:, 1]
    x_float = x_conv.astype(jnp.float32).reshape(shard_len, heads_dev, head_size)
    log_decay = -decay_rate[None, :] * step_size
    cumulative = jnp.cumsum(log_decay, axis=0)
    cumulative_t = cumulative.T
    valid = (segment[:, None] == segment[None, :]) & (row_ids[:, None] >= row_ids[None, :])
    spread = cumulative_t[:, :, None] - cumulative_t[:, None, :]
    decay_matrix = jnp.where(valid[None], jnp.exp(jnp.where(valid[None], spread, 0.0)), 0.0)
    scores = jnp.dot(state_out_proj, state_in_proj.T, precision=highest)
    mixing = decay_matrix * scores[None] * step_size.T[:, None, :]
    y_local = jnp.einsum("hts,shp->thp", mixing, x_float, precision=highest)
    before_pos = seq_index * shard_len - 1
    seg_before = jnp.sum((bounds <= before_pos).astype(jnp.int32))
    carried = (segment == seg_before).astype(jnp.float32)
    entry_gain = jnp.exp(cumulative) * carried[:, None]
    n_seg = lengths.shape[0]
    end_rows = bounds - 1 - seq_index * shard_len
    inside = (end_rows >= 0) & (end_rows < shard_len)
    target_rows = jnp.concatenate([end_rows, jnp.full((1,), shard_len - 1, jnp.int32)])
    target_seg = jnp.concatenate([jnp.arange(n_seg, dtype=jnp.int32), segment[shard_len - 1 :]])
    target_ok = jnp.concatenate([inside, jnp.ones((1,), bool)])
    picker = (row_ids[None, :] == target_rows[:, None]).astype(jnp.float32)
    cum_end = jnp.dot(picker, cumulative, precision=highest)
    reach = (
        target_ok[:, None]
        & (row_ids[None, :] <= target_rows[:, None])
        & (segment[None, :] == target_seg[:, None])
    )
    gap_end = cum_end[:, :, None] - cumulative_t[None, :, :]
    end_weight = (
        jnp.where(reach[:, None, :], jnp.exp(jnp.where(reach[:, None, :], gap_end, 0.0)), 0.0)
        * step_size.T[None]
    )
    states = jnp.einsum("khs,shp,sn->khpn", end_weight, x_float, state_in_proj, precision=highest)
    end_local = states[:n_seg]
    shard_state = states[n_seg]
    end_gain = jnp.where((target_ok & (target_seg == seg_before))[:, None], jnp.exp(cum_end), 0.0)
    shard_gain = end_gain[n_seg]
    end_gain_seg = end_gain[:n_seg]
    gathered = (
        lax.all_gather(shard_gain[None], "seq", axis=0, tiled=True),
        lax.all_gather(shard_state[None], "seq", axis=0, tiled=True),
        lax.all_gather(end_gain_seg[None], "seq", axis=0, tiled=True),
        lax.all_gather(end_local[None], "seq", axis=0, tiled=True),
    )
    gains_all, states_all, egains_all, elocal_all = gathered

    def fold_step(carry, item):
        gain_now, state_now = item
        return (gain_now[:, None, None] * carry + state_now, carry)

    last_state, incoming = lax.scan(
        fold_step, jnp.zeros(shard_state.shape, jnp.float32), (gains_all, states_all)
    )
    state_entry = lax.dynamic_index_in_dim(incoming, seq_index, 0, keepdims=False)
    final_states = jnp.sum(elocal_all + egains_all[:, :, :, None, None] * incoming[:, None], axis=0)
    y_entry = (
        jnp.einsum("tn,hpn->thp", state_out_proj, state_entry, precision=highest)
        * entry_gain[:, :, None]
    )
    y_total = y_local + y_entry + skip_gain[None, :, None] * x_float
    gate_values = jax.nn.silu(gate_in.astype(jnp.float32)).reshape(shard_len, heads_dev, head_size)
    gated = (y_total * gate_values).reshape(shard_len, width_zx).astype(jnp.bfloat16)
    mixed = lax.psum_scatter(
        jnp.dot(gated, proj_out, preferred_element_type=jnp.float32),
        "tensor",
        scatter_dimension=0,
        tiled=True,
    )
    return (mixed.astype(jnp.bfloat16), final_states)


def solution(mesh):
    in_specs = (
        P(("seq", "tensor"), None),
        P(),
        P(None, None, "tensor"),
        P(None, None, "tensor"),
        P(None, "tensor"),
        P(None, "tensor"),
        P(None, None, "tensor"),
        P("tensor"),
        P(None, "tensor"),
        P("tensor"),
        P("tensor"),
        P("tensor"),
        P("tensor", None),
    )
    out_specs = (P(("seq", "tensor"), None), P(None, "tensor", None, None))
    return jax.shard_map(body, mesh=mesh, in_specs=in_specs, out_specs=out_specs, check_vma=False)
```

profile of v0, /device:TPU:0, one launch (start us, length us, event | category | flops | bytes accessed | tf_op | source)
XLA Modules:
  0.0 207.5 jit_solution(12037769887396977083)
XLA Ops:
  7.2 0.0 copy-start
  7.2 0.0 all-gather.7.cloned.1.call-start
  7.2 0.7 all-gather.7.cloned.1.call-update
  7.9 0.0 all-gather.9.cloned.1.call-start
  8.0 0.0 copy-start.15
  8.0 0.0 copy-start.16
  8.1 9.3 %copy.64 = bf16[512,8,2,512]{3,1,2,0:T(8,128)(2,1)} copy(bf16[512,8,2,512]{3,2,1,0:T(2,128)(2,1)} %bitcast.74) | data formatting | bytes 16777216
  17.4 0.2 reduce-window.14
  17.6 0.1 reshape.254
  17.7 0.1 reshape.253
  17.8 0.1 fusion.47
  17.9 0.6 slice.81
  18.5 0.1 pad_add_fusion.2
  18.5 0.6 fusion.52
  19.2 1.4 compare_and_fusion
  20.6 0.7 compare_convert_fusion.1
  21.3 0.1 fusion.50
  21.4 32.9 %all-gather.7.cloned.1.call-done = bf16[256,4096]{1,0:T(8,128)(2,1)} async-done(((bf16[16,4096]{1,0:T(8,128)(2,1)}), bf16[256,4096]{1,0:T(8,128)(2,1)}) %all-gather.7.cloned.1.call-update) | async-done | bytes 2097168 | tf_op jit(solution)/shard_map/all_gather | solution.py:61
  54.3 6.5 %convolution_convert_fusion = bf16[256,1024]{1,0:T(8,128)(2,1)S(1)} fusion(bf16[256,4096]{1,0:T(8,128)(2,1)} %all-gather.7.cloned.1.call-done, bf16[4096,1024]{1,0:T(8,128)(2,1)} %bitcast.75), kind=kOutput, calls=%fused_computation.17 | convolution fusion | flops 2147745792 | bytes 11010048 | tf_op jit(solution)/shard_map/dot_general | solution.py:64
  60.9 0.8 convolution_convert_fusion.1
  61.7 3.4 %collective-permute-start = (bf16[3,640]{1,0:T(4,128)(2,1)S(1)}, bf16[3,640]{1,0:T(4,128)(2,1)S(1)}, u32[]{:S(2)}, u32[]{:S(2)}) collective-permute-start(bf16[3,640]{1,0:T(4,128)(2,1)S(1)} %pad_maximum_fusion.1), channel_id=1, source_target_pairs={{0,16},{1,17},{2,18},{3,19},{4,20},{5,21},{6,22},{7,23},{8,24},{9,... | collective-permute-start | bytes 11528 | tf_op jit(solution)/shard_map/ppermute | solution.py:18
  65.1 0.7 compare_select_fusion
  65.7 0.1 multiply_bitcast_fusion.2
  65.8 0.6 reduce-window.18
  66.4 0.2 slice_reduce_fusion
  66.6 0.1 multiply_bitcast_fusion.1
  66.7 0.8 exponential_select_fusion
  67.5 0.1 copy.55
  67.6 0.6 multiply_convert_fusion
  68.2 0.1 copy.51
  68.3 0.1 copy.53
  68.5 0.1 collective-permute-start.1
  68.5 0.7 multiply_bitcast_fusion
  69.3 0.1 copy.50
  69.5 0.4 collective-permute-done.1
  69.9 0.1 maximum_select_fusion
  70.0 2.7 %fusion.12 = f32[7,8,64,128]{3,2,0,1:T(8,128)S(1)} fusion(f32[256,8,7]{0,2,1:T(8,128)} %multiply_bitcast_fusion, f32[256,8,64]{0,2,1:T(8,128)S(1)} %convert.14, bf16[256,2,128]{2,0,1:T(8,128)(2,1)S(1)} %maximum_select_fusion), kind=kOutput, calls=%fused_computation.16 | convolution fusion | flops 1410203648 | bytes 2482176 | tf_op jit(solution)/shard_map/khs,shp,sn->khpn/dot_general | solution.py:131
  72.7 1.2 slice.104
  74.0 0.0 all-gather.9.cloned.1.call-update
  74.0 0.0 reduce-scatter.2.cloned.1.call-start
  74.0 1.4 fusion.36
  75.5 1.2 slice_bitcast_fusion.1
  76.6 4.6 %all-gather.2 = f32[2,1,8]{2,1,0:T(1,128)} all-gather(f32[1,1,8]{2,1,0:T(1,128)} %slice_bitcast_fusion.1), channel_id=1, replica_groups=mesh['seq'=2,'tensor'=16] {'seq'}, dimensions={0}, use_global_device_ids=true | all-gather | bytes 96 | tf_op jit(solution)/shard_map/all_gather | solution.py:138
  81.2 1.9 convert_multiply_fusion
  83.2 2.1 copy.57
  85.3 15.0 %all_gather.17 = f32[2,8,64,128]{3,2,0,1:T(8,128)S(1)} all-gather(f32[1,8,64,128]{3,2,0,1:T(8,128)S(1)} %slice.102), channel_id=1, replica_groups=mesh['seq'=2,'tensor'=16] {'seq'}, dimensions={0}, use_global_device_ids=true | all-gather | bytes 786432 | tf_op jit(solution)/shard_map/all_gather | solution.py:139
  100.2 0.2 fusion.39
  100.4 3.5 %fusion.15 = f32[256,8,64]{0,2,1:T(8,128)} fusion(bf16[256,8,64]{0,2,1:T(8,128)(2,1)S(1)} %bitcast.78, f32[8,256]{1,0:T(8,128)S(1)} %compare_select_fusion, f32[256,256]{1,0:T(8,128)S(1)} %fusion.39, f32[8,256]{1,0:T(8,128)} %copy-done.6, pred[256,256]{1,0:T(8,128)(4,1)} %fusion.36), kind=kOutput, calls=%fused_computation.18 | convolution fusion | flops 405274624 | bytes 1130496 | tf_op jit(solution)/shard_map/hts,shp->thp/dot_general | solution.py:108
  104.0 1.6 while.13
  104.0 0.7 fusion.68
  104.7 0.1 bitcast_add_fusion.2
  104.8 0.6 fusion.68
  105.4 0.1 bitcast_add_fusion.2
  105.6 1.4 fusion.21
  107.0 5.4 %fusion.55 = f32[256,4096]{1,0:T(8,128)} fusion(bf16[256,512]{0,1:T(8,128)(2,1)S(1)} %bitcast.81, bf16[512,4096]{1,0:T(8,128)(2,1)} %param.27), kind=kOutput, calls=%fused_computation.103 | convolution fusion | flops 1073741824 | bytes 8650752 | tf_op jit(solution)/shard_map/dot_general | solution.py:162
  112.4 0.0 reduce-scatter.2.cloned.1.call-update
  112.5 0.7 copy-done.10
  113.1 4.4 %all-gather.3 = f32[2,6,8]{2,1,0:T(8,128)S(1)} all-gather(f32[1,6,8]{2,1,0:T(8,128)S(1)} %slice_bitcast_fusion), channel_id=3, replica_groups=mesh['seq'=2,'tensor'=16] {'seq'}, dimensions={0}, use_global_device_ids=true | all-gather | bytes 576 | tf_op jit(solution)/shard_map/all_gather | solution.py:140
  117.5 0.1 copy.58
  117.6 5.5 %all-gather.9.cloned.1.call-done = f32[12,8,64,128]{3,2,0,1:T(8,128)} async-done(((f32[6,8,64,128]{3,2,0,1:T(8,128)}), f32[12,8,64,128]{3,2,0,1:T(8,128)}) %all-gather.9.cloned.1.call-update) | async-done | bytes 3145744 | tf_op jit(solution)/shard_map/all_gather | solution.py:141
  123.1 2.5 %add_reduce_fusion = f32[6,8,64,128]{3,2,0,1:T(8,128)S(1)} fusion(f32[2,6,8,64,128]{4,3,1,0,2:T(8,128)} %bitcast.76, f32[2,6,8]{1,0,2:T(2,128)S(1)} %copy.58, f32[2,8,64,128]{3,2,1,0:T(8,128)S(1)} %get-tuple-element.29), kind=kLoop, calls=%fused_computation.6 | loop fusion | flops 1966080 | bytes 5243264 | tf_op jit(solution)/shard_map/reduce_sum | solution.py:153
  125.6 1.3 copy.60
  127.0 72.4 %reduce-scatter.2.cloned.1.call-done = f32[16,4096]{1,0:T(8,128)} async-done(((f32[256,4096]{1,0:T(8,128)}), f32[16,4096]{1,0:T(8,128)}) %reduce-scatter.2.cloned.1.call-update) | async-done | bytes 262160 | tf_op jit(solution)/shard_map/reduce_scatter | solution.py:161
  199.4 1.6 convert_element_type.88
  (53 shorter events, 0.4 us)
Async XLA Ops:
  7.2 53.6 %copy-start = (bf16[4096,2,64]{0,2,1:T(8,128)(2,1)S(1)}, bf16[4096,2,64]{0,2,1:T(8,128)(2,1)}, u32[]{:S(2)}) copy-start(bf16[4096,2,64]{0,2,1:T(8,128)(2,1)} %param.18) | copy-start | bytes 3145732
  7.2 47.1 %all-gather.7.cloned.1.call-start = ((), (), s32[]{:S(2)}) async-start(), calls=%async_computation.1 | async-start | bytes 2228224 | tf_op jit(solution)/shard_map/all_gather | solution.py:61
  7.9 115.2 %all-gather.9.cloned.1.call-start = ((), (), s32[]{:S(2)}) async-start(), calls=%async_computation.3 | async-start | bytes 4718592 | tf_op jit(solution)/shard_map/all_gather | solution.py:141
  8.0 9.4 %copy-start.15 = (s32[6]{0:T(128)S(1)}, s32[6]{0:T(128)}, u32[]{:S(2)}) copy-start(s32[6]{0:T(128)} %param.16) | copy-start | bytes 76
  8.0 9.6 %copy-start.9 = (f32[4,2,64]{2,1,0:T(2,128)S(1)}, f32[4,2,64]{2,1,0:T(2,128)}, u32[]{:S(2)}) copy-start(f32[4,2,64]{2,1,0:T(2,128)} %param.21) | copy-start | bytes 6148
  8.0 9.7 %copy-start.14 = (f32[2,64]{1,0:T(2,128)S(1)}, f32[2,64]{1,0:T(2,128)}, u32[]{:S(2)}) copy-start(f32[2,64]{1,0:T(2,128)} %param.23) | copy-start | bytes 1540
  8.0 9.7 %copy-start.16 = (f32[8]{0:T(128)S(1)}, f32[8]{0:T(128)}, u32[]{:S(2)}) copy-start(f32[8]{0:T(128)} %param.25) | copy-start | bytes 100
  8.0 12.5 %copy-start.8 = (f32[4,512]{1,0:T(4,128)S(1)}, f32[4,512]{1,0:T(4,128)}, u32[]{:S(2)}) copy-start(f32[4,512]{1,0:T(4,128)} %param.20) | copy-start | bytes 24580
  8.1 12.5 %copy-start.11 = (f32[512]{0:T(512)S(1)}, f32[512]{0:T(512)}, u32[]{:S(2)}) copy-start(f32[512]{0:T(512)} %param.22) | copy-start | bytes 6148
  17.9 3.4 %copy-start.7 = (s32[256]{0:T(256)}, s32[256]{0:T(256)S(1)}, u32[]{:S(2)}) copy-start(s32[256]{0:T(256)S(1)} %get-tuple-element.76) | copy-start | bytes 3076
  54.3 6.5 %copy-start.1 = (bf16[256,4096]{1,0:T(8,128)(2,1)S(1)}, bf16[256,4096]{1,0:T(8,128)(2,1)}, u32[]{:S(2)}) copy-start(bf16[256,4096]{1,0:T(8,128)(2,1)} %all-gather.7.cloned.1.call-done) | copy-start | bytes 6291460
  60.8 6.7 %copy-start.2 = (bf16[256,1024]{1,0:T(8,128)(2,1)}, bf16[256,1024]{1,0:T(8,128)(2,1)S(1)}, u32[]{:S(2)}) copy-start(bf16[256,1024]{1,0:T(8,128)(2,1)S(1)} %convolution_convert_fusion) | copy-start | bytes 1572868
  60.8 4.2 %copy-start.5 = (bf16[4096,8]{0,1:T(8,128)(2,1)S(1)}, bf16[4096,8]{0,1:T(8,128)(2,1)}, u32[]{:S(2)}) copy-start(bf16[4096,8]{0,1:T(8,128)(2,1)} %param.19) | copy-start | bytes 196612
  60.8 4.2 %copy-start.12 = (f32[8]{0:T(128)S(1)}, f32[8]{0:T(128)}, u32[]{:S(2)}) copy-start(f32[8]{0:T(128)} %param.24) | copy-start | bytes 100
  61.7 5.9 %collective-permute-start = (bf16[3,640]{1,0:T(4,128)(2,1)S(1)}, bf16[3,640]{1,0:T(4,128)(2,1)S(1)}, u32[]{:S(2)}, u32[]{:S(2)}) collective-permute-start(bf16[3,640]{1,0:T(4,128)(2,1)S(1)} %pad_maximum_fusion.1), channel_id=1, source_target_pairs={{0,16},{1,17},{2,18},{3,19},{4,20},{5,21},{6,22},{7,23},{8,24},{9,... | collective-permute-start | bytes 11528 | tf_op jit(solution)/shard_map/ppermute | solution.py:18
  66.7 3.2 %copy-start.6 = (f32[8,256]{1,0:T(8,128)}, f32[8,256]{1,0:T(8,128)S(1)}, u32[]{:S(2)}) copy-start(f32[8,256]{1,0:T(8,128)S(1)} %get-tuple-element.93) | copy-start | bytes 24580
  68.5 1.4 collective-permute-start.1
  74.0 125.4 %reduce-scatter.2.cloned.1.call-start = ((), (), s32[]{:S(2)}) async-start(), calls=%async_computation.2 | async-start | bytes 4456448 | tf_op jit(solution)/shard_map/reduce_scatter | solution.py:161
  100.4 3.5 %copy-start.4 = (f32[2,8,64,128]{3,2,1,0:T(8,128)S(1)}, f32[2,8,64,128]{3,2,1,0:T(8,128)}, u32[]{:S(2)}) copy-start(f32[2,8,64,128]{3,2,1,0:T(8,128)} %custom-call.2) | copy-start | bytes 1572868
  104.0 1.6 copy-start.3
  104.0 1.6 copy-start.13
  112.4 0.7 copy-start.10
Sparse Core Ops, SparseCore 0:
  10.2 44.0 all-gather.6
  74.1 48.9 all-gather.8
  127.0 72.3 reduce-scatter.1
where the time goes:
time: 208 us
  waiting for transfers between devices  112 us (54%)
  blocking collectives  24 us (12%)
  matrix products  22 us (11%)
  local copies, waits for them, and re-layouts  18.7 us (9%)
  between operations  14.1 us (7%)
  other arithmetic  13.1 us (6%)
  starting transfers between devices  3.56 us (2%)
    reduce_scatter x1, waiting for transfers between devices, body(): lax.psum_scatter(jnp.dot(gated, proj_out, preferred_element_type=jnp.floa...  72.4 us
    all_gather x1, waiting for transfers between devices, body(): piece = lax.all_gather(tokens, 'tensor', axis=0, tiled=True)  32.9 us
    all_gather x1, blocking collectives, body(): lax.all_gather(shard_state[None], 'seq', axis=0, tiled=True)  15 us
    unnamed x39, local copies, waits for them, and re-layouts  12.6 us
    dot_general x1, matrix products, body(): jnp.dot(piece, zx_flat, preferred_element_type=jnp.float32)  6.49 us
    all_gather x1, waiting for transfers between devices, body(): lax.all_gather(end_local[None], 'seq', axis=0, tiled=True)  5.54 us
    dot_general x1, matrix products, body(): jnp.dot(gated, proj_out, preferred_element_type=jnp.float32)  5.4 us
    all_gather x1, blocking collectives, body(): lax.all_gather(shard_gain[None], 'seq', axis=0, tiled=True)  4.62 us
  transfers between devices with their start and end apart: 5, of which 4 were waited for; matrix products, arithmetic and copies ran while one was open for 19% of the time, Pallas kernels for 0%

commit v1 on v0

--- a/solution.py
+++ b/solution.py
@@ -1,6 +1,8 @@
 import jax
 import jax.numpy as jnp
 from jax import lax
+from jax.experimental import pallas as pl
+from jax.experimental.pallas import tpu as pltpu
 from jax.sharding import PartitionSpec as P
 
 GROUPS = 8
@@ -167,6 +169,466 @@
     return (mixed.astype(jnp.bfloat16), final_states)
 
 
+F32 = jnp.float32
+BF16 = jnp.bfloat16
+ROWS = 16
+LEN = 256
+WIDE = 4096
+CHAN = 512
+STATES = 128
+HIGH = lax.Precision.HIGHEST
+NT = (((1,), (1,)), ((), ()))
+TN = (((0,), (0,)), ((), ()))
+
+
+def remote(src, dst, send, recv, **device):
+    return pltpu.make_async_remote_copy(
+        src_ref=src,
+        dst_ref=dst,
+        send_sem=send,
+        recv_sem=recv,
+        device_id=device,
+        device_id_type=pl.DeviceIdType.MESH,
+    )
+
+
+def segment_of(bounds, pos):
+    total = jnp.zeros(pos.shape, jnp.int32)
+    for bound in bounds:
+        total = total + (bound <= pos).astype(jnp.int32)
+    return total
+
+
+def layer_kernel(
+    lengths,
+    tok_in,
+    zx_in,
+    bc_in,
+    dt_in,
+    taps_x,
+    taps_bc,
+    dt_bias,
+    rate,
+    skip,
+    out_in,
+    mixed,
+    finals,
+    tok,
+    zx_raw,
+    w_zx,
+    w_bc,
+    w_out,
+    t_bc,
+    gate,
+    ext,
+    act,
+    steps,
+    fin,
+    acc,
+    keep,
+    send_a,
+    recv_a,
+    send_b,
+    recv_b,
+    send_c,
+    recv_c,
+    load_sem,
+    zx_sem,
+    agz_s,
+    agz_r,
+    agy_s,
+    agy_r,
+    agc_s,
+    agc_r,
+    misc_s,
+    misc_r,
+    rsa_s,
+    rsa_r,
+    rsb_s,
+    rsb_r,
+    rsc_s,
+    rsc_r,
+):
+    s = lax.axis_index("seq")
+    me = lax.axis_index("tensor")
+    z = me // 4
+    y = (me // 2) % 2
+    c = me % 2
+    oy = 1 - y
+    oc = 1 - c
+    sib = z * 4 + y * 2 + oc
+    ypal = z * 4 + oy * 2 + c
+    zpal = [((z + d) % 4) * 4 + y * 2 + c for d in range(4)]
+    other = 1 - s
+
+    own = pltpu.make_async_copy(tok_in, tok.at[z, y, c], load_sem.at[0])
+    own.start()
+    zx_loads = []
+    for i in range(4):
+        rows = pl.ds(i * 1024, 1024)
+        load = pltpu.make_async_copy(zx_in.at[rows], zx_raw.at[rows], zx_sem.at[i])
+        load.start()
+        zx_loads.append(load)
+    bc_load = pltpu.make_async_copy(bc_in, w_bc.at[:, c], load_sem.at[1])
+    bc_load.start()
+    tap_load = pltpu.make_async_copy(taps_bc, t_bc.at[c], load_sem.at[2])
+    tap_load.start()
+    out_load = pltpu.make_async_copy(out_in, w_out, load_sem.at[3])
+    out_load.start()
+
+    barrier = pltpu.get_barrier_semaphore()
+    for pal in [sib, ypal] + zpal[1:]:
+        pl.semaphore_signal(
+            barrier, inc=1, device_id={"tensor": pal}, device_id_type=pl.DeviceIdType.MESH
+        )
+    pl.semaphore_signal(
+        barrier, inc=1, device_id={"seq": other}, device_id_type=pl.DeviceIdType.MESH
+    )
+    pl.semaphore_wait(barrier, 6)
+
+    started = []
+
+    def go(copy):
+        copy.start()
+        started.append(copy)
+        return copy
+
+    def block(d, yy, cc):
+        return tok.at[(z + 4 - d) % 4, yy, cc]
+
+    here = tok.at[z, y, c]
+    ysend = [go(remote(tok_in, here, agy_s.at[0], agy_r.at[0], tensor=ypal))]
+    zsend = [None]
+    for d in (1, 2, 3):
+        zsend.append(go(remote(tok_in, here, agz_s.at[d], agz_r.at[d], tensor=zpal[d])))
+    csend = {0: go(remote(tok_in, here, agc_s.at[0], agc_r.at[0], tensor=sib))}
+    bc_send = go(remote(bc_in, w_bc.at[:, c], misc_s.at[0], misc_r.at[0], tensor=sib))
+    tap_send = go(remote(taps_bc, t_bc.at[c], misc_s.at[1], misc_r.at[1], tensor=sib))
+
+    def split(i):
+        zx_loads[i].wait()
+
+        @pl.loop(0, 8)
+        def _(j):
+            rows = pl.ds(pl.multiple_of(i * 1024 + j * 128, 128), 128)
+            pair = pltpu.einshape("abc->bac", zx_raw[rows])
+            w_zx[rows, :CHAN] = pair[0]
+            w_zx[rows, CHAN:] = pair[1]
+
+    for d in (1, 3, 2):
+        zsend[d].wait_recv()
+        mine = block(d, y, c)
+        go(remote(mine, mine, agy_s.at[d], agy_r.at[d], tensor=ypal))
+        go(remote(mine, mine, agc_s.at[d], agc_r.at[d], tensor=sib))
+        if d != 2:
+            split(0 if d == 1 else 1)
+    for d in (0, 1, 3, 2):
+        theirs = block(d, oy, c)
+        remote(theirs, theirs, agy_s.at[d], agy_r.at[d], tensor=ypal).wait_recv()
+        go(remote(theirs, theirs, agc_s.at[4 + d], agc_r.at[4 + d], tensor=sib))
+        if d == 0:
+            split(2)
+        if d == 1:
+            split(3)
+    own.wait()
+    bc_load.wait()
+    tap_load.wait()
+    bc_send.wait_recv()
+    tap_send.wait_recv()
+    for d in range(4):
+        for k, yy in ((0, y), (4, oy)):
+            blk = block(d, yy, oc)
+            remote(blk, blk, agc_s.at[k + d], agc_r.at[k + d], tensor=sib).wait_recv()
+
+    def stream():
+        return tok[...].reshape(LEN, WIDE)
+
+    for i in range(2):
+        cols = slice(CHAN + i * 256, CHAN + i * 256 + 256)
+        ext[16:, i * 256 : i * 256 + 256] = jnp.dot(
+            stream(), w_zx[:, cols], preferred_element_type=F32
+        ).astype(BF16)
+    ext[16:, CHAN:] = lax.dot_general(
+        stream(), w_bc[...].reshape(256, WIDE), NT, preferred_element_type=F32
+    ).astype(BF16)
+    halo = go(
+        remote(ext.at[pl.ds(256, 16)], ext.at[pl.ds(0, 16)], misc_s.at[2], misc_r.at[2], seq=other)
+    )
+    dt_raw = lax.dot_general(dt_in[...], stream(), NT, preferred_element_type=F32)
+    dt_raw = dt_raw + dt_bias[...]
+    steps[s] = jax.nn.softplus(dt_raw)
+    step_send = go(remote(steps.at[s], steps.at[s], misc_s.at[3], misc_r.at[3], seq=other))
+    for i in range(2):
+        cols = slice(i * 256, i * 256 + 256)
+        gate[:, cols] = jnp.dot(stream(), w_zx[:, cols], preferred_element_type=F32).astype(BF16)
+
+    n_seg = lengths.shape[0]
+    bounds = []
+    run = jnp.int32(0)
+    for k in range(n_seg):
+        run = run + lengths[k]
+        bounds.append(run)
+    base = s * LEN
+    pos = lax.broadcasted_iota(jnp.int32, (LEN, 128), 0) + base
+    seg_start = jnp.zeros((LEN, 128), jnp.int32)
+    for bound in bounds:
+        seg_start = jnp.where(bound <= pos, jnp.maximum(seg_start, bound), seg_start)
+    masks = [(pos - j >= seg_start).astype(F32) for j in range(4)]
+
+    halo.wait_recv()
+
+    def taps_for(i, row):
+        if i < 4:
+            return taps_x[row : row + 1, i * 128 : i * 128 + 128]
+        lo = (i - 4) * 64
+        return jnp.concatenate(
+            [t_bc[0, row : row + 1, lo : lo + 64], t_bc[1, row : row + 1, lo : lo + 64]], axis=1
+        )
+
+    for i in range(6):
+        cols = slice(i * 128, i * 128 + 128)
+        v = ext[:, cols].astype(F32)
+        total = jnp.zeros((LEN, 128), F32) + taps_for(i, 4)
+        for j in range(4):
+            lagged = v if j == 0 else pltpu.roll(v, j, 0)
+            total = total + taps_for(i, j) * lagged[16:] * masks[j]
+        act[s, :, cols] = (total * lax.logistic(total)).astype(BF16)
+    act_send = go(
+        remote(
+            act.at[s, :, pl.ds(0, 640)],
+            act.at[s, :, pl.ds(0, 640)],
+            misc_s.at[4],
+            misc_r.at[4],
+            seq=other,
+        )
+    )
+
+    ri = lax.broadcasted_iota(jnp.int32, (LEN, LEN), 0)
+    ci = lax.broadcasted_iota(jnp.int32, (LEN, LEN), 1)
+    upper = (ri <= ci).astype(F32)
+    head_of = lax.broadcasted_iota(jnp.int32, (8, CHAN), 1) // 64
+    spread = (head_of == lax.broadcasted_iota(jnp.int32, (8, CHAN), 0)).astype(F32)
+
+    def cumulate(dt):
+        return jnp.dot(-rate[...] * dt, upper, precision=HIGH, preferred_element_type=F32)
+
+    def widen(rows):
+        return lax.dot_general(rows, spread, TN, precision=HIGH, preferred_element_type=F32)
+
+    dt_own = steps[s]
+    cum_r = cumulate(dt_own)
+    cum_c = cum_r.T
+    seg_r = segment_of(bounds, ci + base)
+    seg_c = segment_of(bounds, ri + base)
+    valid = (seg_r == seg_c) & (ri >= ci)
+    b_own = act[s, :, CHAN : CHAN + STATES]
+    c_own = act[s, :, CHAN + STATES :]
+    scores = lax.dot_general(c_own, b_own, NT, preferred_element_type=F32)
+    scores = jnp.where(valid, scores, 0.0)
+    lane = lax.broadcasted_iota(jnp.int32, (LEN, 128), 1)
+    for g in range(4):
+        cols = slice(g * 128, g * 128 + 128)
+        x_pair = act[s, :, cols]
+        halves = []
+        for h in (2 * g, 2 * g + 1):
+            gap = cum_c[:, h : h + 1] - cum_r[h : h + 1, :]
+            mix = jnp.exp(jnp.where(valid, gap, 0.0)) * scores * dt_own[h : h + 1, :]
+            halves.append(jnp.dot(mix.astype(BF16), x_pair, preferred_element_type=F32))
+        acc[:, cols] = jnp.where(lane < 64, halves[0], halves[1])
+
+    step_send.wait_recv()
+    act_send.wait_recv()
+    dt_0 = steps[0]
+    cum_0 = cumulate(dt_0)
+    end_0 = jnp.sum(-rate[...] * dt_0, axis=1, keepdims=True)
+    seg_before = segment_of(bounds, jnp.full((8, LEN), LEN - 1, jnp.int32))
+    place = lax.broadcasted_iota(jnp.int32, (8, LEN), 1)
+    seg_0 = segment_of(bounds, place)
+    seg_1 = segment_of(bounds, place + LEN)
+    seg_own = segment_of(bounds, place + base)
+    last_0 = cum_0[:, LEN - 1 :]
+    into = jnp.exp(last_0 - cum_0) * dt_0 * (seg_0 == seg_before).astype(F32)
+    x_0 = act[0, :, :CHAN].astype(F32)
+    x_in = (x_0 * widen(into)).astype(BF16)
+    entry = lax.dot_general(
+        act[0, :, CHAN : CHAN + STATES], x_in, TN, preferred_element_type=F32
+    ).astype(BF16)
+    carried = ((seg_own == seg_before) & (s > 0)).astype(F32)
+    gain = widen(jnp.exp(cum_r) * carried)
+    y_all = acc[:, :CHAN] + jnp.dot(c_own, entry, preferred_element_type=F32) * gain
+    y_all = y_all + skip[...] * act[s, :, :CHAN].astype(F32)
+    gate_f = gate[...].astype(F32)
+    gate[...] = (y_all * (gate_f * lax.logistic(gate_f))).astype(BF16)
+    out_load.wait()
+
+    @pl.loop(0, 8)
+    def _(i):
+        cols = pl.ds(pl.multiple_of(i * 512, 512), 512)
+        acc[:, cols] = jnp.dot(gate[...], w_out[:, cols], preferred_element_type=F32)
+
+    def part(d, yy, cc):
+        return pl.ds(pl.multiple_of(((z + d) % 4) * 64 + yy * 32 + cc * 16, 16), 16)
+
+    order = (2, 1, 3, 0)
+    a_copy = {}
+    for d in order:
+        for yy in range(2):
+            send_a[d, yy] = acc[part(d, yy, oc), :].astype(BF16)
+        a_copy[d] = go(
+            remote(send_a.at[d], recv_a.at[d], rsa_s.at[d], rsa_r.at[d], tensor=sib)
+        )
+    b_copy = {}
+    for d in order:
+        a_copy[d].wait_recv()
+        send_b[d] = (acc[part(d, oy, c), :] + recv_a[d, oy].astype(F32)).astype(BF16)
+        b_copy[d] = go(
+            remote(send_b.at[d], recv_b.at[d], rsb_s.at[d], rsb_r.at[d], tensor=ypal)
+        )
+        keep[d] = acc[part(d, y, c), :] + recv_a[d, y].astype(F32)
+
+    def finals_part():
+        dt_1 = steps[1]
+        cum_1 = cumulate(dt_1) + last_0
+        ends_0 = jnp.zeros((8, LEN), F32)
+        ends_1 = jnp.zeros((8, LEN), F32)
+        for k in range(n_seg):
+            spot_0 = (place == bounds[k] - 1).astype(F32) * cum_0
+            spot_1 = (place + LEN == bounds[k] - 1).astype(F32) * cum_1
+            end = jnp.sum(spot_0 + spot_1, axis=1, keepdims=True)
+            ends_0 = jnp.where(seg_0 == k, end, ends_0)
+            ends_1 = jnp.where(seg_1 == k, end, ends_1)
+        w_0 = widen(jnp.exp(ends_0 - cum_0) * dt_0)
+        w_1 = widen(jnp.exp(ends_1 - cum_1) * dt_1)
+        x_1 = act[1, :, :CHAN].astype(F32)
+        xw_0 = (x_0 * w_0).astype(BF16)
+        xw_1 = (x_1 * w_1).astype(BF16)
+        b_0 = act[0, :, CHAN : CHAN + STATES]
+        b_1 = act[1, :, CHAN : CHAN + STATES]
+        spot = lax.broadcasted_iota(jnp.int32, (LEN, STATES), 0)
+        col_0 = segment_of(bounds, spot)
+        col_1 = segment_of(bounds, spot + LEN)
+        for k in range(n_seg):
+            m_0 = jnp.where(col_0 == k, b_0.astype(F32), 0.0).astype(BF16)
+            m_1 = jnp.where(col_1 == k, b_1.astype(F32), 0.0).astype(BF16)
+            fin[k] = lax.dot_general(
+                xw_0, m_0, TN, preferred_element_type=F32
+            ) + lax.dot_general(xw_1, m_1, TN, preferred_element_type=F32)
+
+    c_copy = {}
+    for d in order:
+        b_copy[d].wait_recv()
+        summed = keep[d] + recv_b[d].astype(F32)
+        if d == 0:
+            keep[0] = summed
+        else:
+            send_c[d] = summed.astype(BF16)
+            c_copy[d] = go(
+                remote(send_c.at[d], recv_c.at[d], rsc_s.at[d], rsc_r.at[d], tensor=zpal[d])
+            )
+        if d == 2:
+            finals_part()
+            fin_out = pltpu.make_async_copy(fin, finals, load_sem.at[4])
+            fin_out.start()
+    total = keep[0]
+    for d in (1, 3, 2):
+        c_copy[d].wait_recv()
+        total = total + recv_c[d].astype(F32)
+    mixed[...] = total.astype(BF16)
+    for copy in started:
+        copy.wait_send()
+    fin_out.wait()
+
+
+def fused_body(
+    tokens,
+    lengths,
+    proj_zx,
+    proj_bc,
+    proj_dt,
+    conv_x,
+    conv_bc,
+    bias_x,
+    bias_bc,
+    dt_bias,
+    decay_rate,
+    skip_gain,
+    proj_out,
+):
+    n_seg = lengths.shape[0]
+    bc_view = proj_bc.transpose(1, 2, 0)
+    dt_view = proj_dt.T
+    taps_x = jnp.concatenate([conv_x, bias_x[None], jnp.zeros((3, CHAN), F32)], axis=0)
+    taps_bc = jnp.concatenate(
+        [conv_bc.reshape(4, 128), bias_bc.reshape(1, 128), jnp.zeros((3, 128), F32)], axis=0
+    )
+    any_spec = pl.BlockSpec(memory_space=pl.ANY)
+    vmem = pl.BlockSpec(memory_space=pltpu.VMEM)
+    dma = pltpu.SemaphoreType.DMA
+    mixed, finals = pl.pallas_call(
+        layer_kernel,
+        out_shape=(
+            jax.ShapeDtypeStruct((ROWS, WIDE), BF16),
+            jax.ShapeDtypeStruct((n_seg, CHAN, STATES), F32),
+        ),
+        in_specs=[pl.BlockSpec(memory_space=pltpu.SMEM), any_spec, any_spec, any_spec]
+        + [vmem, vmem, any_spec, vmem, vmem, vmem, any_spec],
+        out_specs=(vmem, any_spec),
+        scratch_shapes=[
+            pltpu.VMEM((4, 2, 2, ROWS, WIDE), BF16),
+            pltpu.VMEM((WIDE, 2, CHAN), BF16),
+            pltpu.VMEM((WIDE, 2 * CHAN), BF16),
+            pltpu.VMEM((2, 2, 64, WIDE), BF16),
+            pltpu.VMEM((CHAN, WIDE), BF16),
+            pltpu.VMEM((2, 8, 128), F32),
+            pltpu.VMEM((LEN, CHAN), BF16),
+            pltpu.VMEM((16 + LEN, CHAN + 256), BF16),
+            pltpu.VMEM((2, LEN, CHAN + 256), BF16),
+            pltpu.VMEM((2, 8, LEN), F32),
+            pltpu.VMEM((n_seg, CHAN, STATES), F32),
+            pltpu.VMEM((LEN, WIDE), F32),
+            pltpu.VMEM((4, ROWS, WIDE), F32),
+            pltpu.VMEM((4, 2, ROWS, WIDE), BF16),
+            pltpu.VMEM((4, 2, ROWS, WIDE), BF16),
+            pltpu.VMEM((4, ROWS, WIDE), BF16),
+            pltpu.VMEM((4, ROWS, WIDE), BF16),
+            pltpu.VMEM((4, ROWS, WIDE), BF16),
+            pltpu.VMEM((4, ROWS, WIDE), BF16),
+            dma((5,)),
+            dma((4,)),
+            dma((4,)),
+            dma((4,)),
+            dma((4,)),
+            dma((4,)),
+            dma((8,)),
+            dma((8,)),
+            dma((5,)),
+            dma((5,)),
+            dma((4,)),
+            dma((4,)),
+            dma((4,)),
+            dma((4,)),
+            dma((4,)),
+            dma((4,)),
+        ],
+        compiler_params=pltpu.CompilerParams(
+            collective_id=0, has_side_effects=True, vmem_limit_bytes=60 << 20
+        ),
+    )(
+        lengths,
+        tokens,
+        proj_zx,
+        bc_view,
+        dt_view,
+        taps_x,
+        taps_bc,
+        dt_bias.reshape(8, 1),
+        decay_rate.reshape(8, 1),
+        jnp.repeat(skip_gain, 64).reshape(1, CHAN),
+        proj_out,
+    )
+    return (mixed, finals.reshape(n_seg, 8, 64, STATES))
+
+
 def solution(mesh):
     in_specs = (
         P(("seq", "tensor"), None),
@@ -184,4 +646,6 @@
         P("tensor", None),
     )
     out_specs = (P(("seq", "tensor"), None), P(None, "tensor", None, None))
-    return jax.shard_map(body, mesh=mesh, in_specs=in_specs, out_specs=out_specs, check_vma=False)
+    small = mesh.shape["seq"] == 2 and mesh.shape["tensor"] == 16
+    chosen = fused_body if small else body
+    return jax.shard_map(chosen, mesh=mesh, in_specs=in_specs, out_specs=out_specs, check_vma=False)

time: 208 us -> 76.7 us (0.37)
  waiting for transfers between devices: 112 us -> 0 us
  Pallas kernels: 0 us -> 63.8 us
  blocking collectives: 24 us -> 0 us
  matrix products: 22 us -> 0 us
  between operations: 14.1 us -> 0.64 us
  other arithmetic: 13.1 us -> 2.05 us
  local copies, waits for them, and re-layouts: 18.7 us -> 9.91 us
  starting transfers between devices: 3.56 us -> 0 us
    reduce_scatter x1 -> x0, waiting for transfers between devices: 72.4 us -> none  [body(): lax.psum_scatter(jnp.dot(gated, proj_out, preferred_element_type=jnp.floa...]
    pallas_call x0 -> x1, Pallas kernels: none -> 63.8 us  [fused_body(): pl.pallas_call(layer_kernel, out_shape=(jax.ShapeDtypeStruct((ROWS, WIDE)...]
    all_gather x2 -> x0, waiting for transfers between devices: 38.5 us -> none  [the longest x1 32.9 us: body(): piece = lax.all_gather(tokens, 'tensor', axis=0, tiled=True)]
    all_gather x3 -> x0, blocking collectives: 24 us -> none  [the longest x1 15 us: body(): lax.all_gather(shard_state[None], 'seq', axis=0, tiled=True)]
    dot_general x9 -> x0, matrix products: 22 us -> none  [the longest x1 6.49 us: body(): jnp.dot(piece, zx_flat, preferred_element_type=jnp.float32)]
    unnamed x39 -> x2, local copies, waits for them, and re-layouts: 12.6 us -> 4.29 us
    reshape x3 -> x4, local copies, waits for them, and re-layouts: 0.28 us -> 4.16 us  [the longest x1 1.32 us: fused_body(): decay_rate.reshape(8, 1)]
    ppermute x2 -> x0, starting transfers between devices: 3.44 us -> none  [the longest x1 3.37 us: passed_along(): return lax.ppermute(block, axis, route)]
  transfers between devices with their start and end apart: 5 -> 0, of which waited for: 4 -> 0; matrix products, arithmetic and copies ran while one was open for 19% -> 0% of each run, Pallas kernels for 0% -> 0%
where the time goes in v1:
time: 76.7 us; the launch traced here: 76.4 us
  Pallas kernels  63.8 us (83%)
  local copies, waits for them, and re-layouts  9.91 us (13%)
  other arithmetic  2.05 us (3%)
    pallas_call x1, Pallas kernels, fused_body(): pl.pallas_call(layer_kernel, out_shape=(jax.ShapeDtypeStruct((ROWS, WIDE)...  63.8 us
    unnamed x2, local copies, waits for them, and re-layouts  4.29 us

profile of v1, /device:TPU:0, one launch (start us, length us, event | category | flops | bytes accessed | tf_op | source)
XLA Modules:
  0.0 76.4 jit_solution(13369597483561163384)
XLA Ops:
  0.6 0.8 reshape.20
  1.4 0.1 pad.5.clone
  1.5 0.8 %reshape.19 = f32[4,128]{1,0:T(4,128)S(1)} reshape(f32[4,2,64]{2,1,0:T(2,128)} %param.19) | data formatting | bytes 4096 | tf_op jit(solution)/shard_map/reshape | solution.py:562
  2.2 0.7 maximum_maximum_fusion.1.taps_bc
  2.9 1.3 %copy.15.dt_bias = f32[8,1]{1,0:T(8,128)} copy(f32[8,1]{0,1:T(1,128)} %bitcast.10) | data formatting | bytes 64 | tf_op jit(solution)/shard_map/reshape | solution.py:624
  4.2 1.3 %copy.16.rate = f32[8,1]{1,0:T(8,128)} copy(f32[8,1]{0,1:T(1,128)} %bitcast.11) | data formatting | bytes 64 | tf_op jit(solution)/shard_map/reshape | solution.py:625
  5.5 0.7 broadcast_in_dim.15
  6.3 0.7 reshape_reshape.3.skip
  6.9 1.4 %maximum_maximum_fusion.taps_x = f32[8,512]{1,0:T(8,128)} fusion(f32[1,512]{1,0:T(1,128)} %bitcast.9, f32[4,512]{1,0:T(4,128)} %param.18, f32[8]{0:T(128)S(1)} %pad.5.clone), kind=kLoop, calls=%fused_computation | loop fusion | flops 8192 | bytes 26656 | tf_op jit(solution)/shard_map/concatenate | solution.py:560
  8.3 63.8 %shard_map.140 = (bf16[16,4096]{1,0:T(8,128)(2,1)}, f32[6,512,128]{2,1,0:T(8,128)}) custom-call(s32[6]{0:T(128)} %lengths.1, bf16[16,4096]{1,0:T(8,128)(2,1)} %tok_in.1, bf16[4096,2,512]{2,1,0:T(2,128)(2,1)} %zx_in.1, bf16[2,64,4096]{2,1,0:T(8,128)(2,1)} %bitcast.7, bf16[8,4096]{1,0:T(8,128)(2,1)} %bitcast.8, f32[8,512]{1,0:T(8,128)} %maximum_maximum_fusion.taps_x, ...), custom_call_target="tpu_custom_call" | custom-call | tf_op jit(solution)/shard_map/pallas_call | solution.py:567
  72.1 1.6 %copy.19 = bf16[16,4096]{1,0:T(8,128)(2,1)} copy(bf16[16,4096]{1,0:T(8,128)(2,1)} %get-tuple-element.8) | data formatting | bytes 262144
  73.7 2.7 %copy.20 = f32[6,8,64,128]{3,2,1,0:T(8,128)} copy(f32[6,8,64,128]{3,2,1,0:T(8,128)} %bitcast.6) | data formatting | bytes 3145728
  (1 shorter events, 0.0 us)

commit v2 on v1

--- a/solution.py
+++ b/solution.py
@@ -205,11 +205,13 @@
     zx_in,
     bc_in,
     dt_in,
-    taps_x,
-    taps_bc,
+    conv_x,
+    bias_x,
+    conv_bc,
+    bias_bc,
     dt_bias,
-    rate,
-    skip,
+    rate_in,
+    skip_in,
     out_in,
     mixed,
     finals,
@@ -218,7 +220,8 @@
     w_zx,
     w_bc,
     w_out,
-    t_bc,
+    t_conv,
+    t_bias,
     gate,
     ext,
     act,
@@ -234,14 +237,18 @@
     recv_c,
     load_sem,
     zx_sem,
-    agz_s,
-    agz_r,
+    up_s,
+    up_r,
+    down_s,
+    down_r,
     agy_s,
     agy_r,
     agc_s,
     agc_r,
     misc_s,
     misc_r,
+    act_s,
+    act_r,
     rsa_s,
     rsa_r,
     rsb_s,
@@ -271,8 +278,10 @@
         zx_loads.append(load)
     bc_load = pltpu.make_async_copy(bc_in, w_bc.at[:, c], load_sem.at[1])
     bc_load.start()
-    tap_load = pltpu.make_async_copy(taps_bc, t_bc.at[c], load_sem.at[2])
+    tap_load = pltpu.make_async_copy(conv_bc, t_conv.at[c], load_sem.at[2])
     tap_load.start()
+    off_load = pltpu.make_async_copy(bias_bc, t_bias.at[c], load_sem.at[5])
+    off_load.start()
     out_load = pltpu.make_async_copy(out_in, w_out, load_sem.at[3])
     out_load.start()
 
@@ -293,17 +302,25 @@
         started.append(copy)
         return copy
 
-    def block(d, yy, cc):
-        return tok.at[(z + 4 - d) % 4, yy, cc]
+    def block(zz, yy, cc):
+        return tok.at[(zz + 4) % 4, yy, cc]
+
+    guarded = []
+
+    def maybe(condition, copy):
+        pl.when(condition)(copy.start)
+        guarded.append((condition, copy))
 
     here = tok.at[z, y, c]
-    ysend = [go(remote(tok_in, here, agy_s.at[0], agy_r.at[0], tensor=ypal))]
-    zsend = [None]
-    for d in (1, 2, 3):
-        zsend.append(go(remote(tok_in, here, agz_s.at[d], agz_r.at[d], tensor=zpal[d])))
-    csend = {0: go(remote(tok_in, here, agc_s.at[0], agc_r.at[0], tensor=sib))}
+    above = zpal[1]
+    below = zpal[3]
+    maybe(z < 3, remote(tok_in, here, up_s.at[0], up_r.at[1], tensor=above))
+    maybe(z > 0, remote(tok_in, here, down_s.at[0], down_r.at[1], tensor=below))
+    go(remote(tok_in, here, agy_s.at[z], agy_r.at[z], tensor=ypal))
+    go(remote(tok_in, here, agc_s.at[z], agc_r.at[z], tensor=sib))
     bc_send = go(remote(bc_in, w_bc.at[:, c], misc_s.at[0], misc_r.at[0], tensor=sib))
-    tap_send = go(remote(taps_bc, t_bc.at[c], misc_s.at[1], misc_r.at[1], tensor=sib))
+    tap_send = go(remote(conv_bc, t_conv.at[c], misc_s.at[1], misc_r.at[1], tensor=sib))
+    off_send = go(remote(bias_bc, t_bias.at[c], misc_s.at[5], misc_r.at[5], tensor=sib))
 
     def split(i):
         zx_loads[i].wait()
@@ -315,29 +332,54 @@
             w_zx[rows, :CHAN] = pair[0]
             w_zx[rows, CHAN:] = pair[1]
 
-    for d in (1, 3, 2):
-        zsend[d].wait_recv()
-        mine = block(d, y, c)
-        go(remote(mine, mine, agy_s.at[d], agy_r.at[d], tensor=ypal))
-        go(remote(mine, mine, agc_s.at[d], agc_r.at[d], tensor=sib))
-        if d != 2:
-            split(0 if d == 1 else 1)
-    for d in (0, 1, 3, 2):
-        theirs = block(d, oy, c)
-        remote(theirs, theirs, agy_s.at[d], agy_r.at[d], tensor=ypal).wait_recv()
-        go(remote(theirs, theirs, agc_s.at[4 + d], agc_r.at[4 + d], tensor=sib))
-        if d == 0:
-            split(2)
-        if d == 1:
-            split(3)
+    def relay(k, zz, have, ahead, more, sends, recvs):
+        mine = block(zz, y, c)
+        at = (zz + 4) % 4
+
+        @pl.when(have)
+        def _():
+            remote(mine, mine, sends.at[0], recvs.at[k], tensor=ahead).wait_recv()
+
+        if k < 3:
+            maybe(
+                have & more, remote(mine, mine, sends.at[k], recvs.at[k + 1], tensor=ahead)
+            )
+        maybe(have, remote(mine, mine, agy_s.at[at], agy_r.at[at], tensor=ypal))
+        maybe(have, remote(mine, mine, agc_s.at[at], agc_r.at[at], tensor=sib))
+
+    def across(zz, have):
+        theirs = block(zz, oy, c)
+        at = (zz + 4) % 4
+
+        @pl.when(have)
+        def _():
+            remote(theirs, theirs, agy_s.at[at], agy_r.at[at], tensor=ypal).wait_recv()
+
+        maybe(
+            have, remote(theirs, theirs, agc_s.at[4 + at], agc_r.at[4 + at], tensor=sib)
+        )
+
+    always = z >= 0
+    split(0)
+    for k in (1, 2, 3):
+        relay(k, z - k, z >= k, above, z < 3, up_s, up_r)
+        relay(k, z + k, z + k <= 3, below, z > 0, down_s, down_r)
+        if k == 1:
+            across(z, always)
+        else:
+            across(z - k + 1, z >= k - 1)
+            across(z + k - 1, z + k - 1 <= 3)
+        split(k)
+    across(z - 3, z >= 3)
+    across(z + 3, z + 3 <= 3)
     own.wait()
-    bc_load.wait()
-    tap_load.wait()
-    bc_send.wait_recv()
-    tap_send.wait_recv()
+    for load in (bc_load, tap_load, off_load):
+        load.wait()
+    for sent in (bc_send, tap_send, off_send):
+        sent.wait_recv()
     for d in range(4):
         for k, yy in ((0, y), (4, oy)):
-            blk = block(d, yy, oc)
+            blk = tok.at[d, yy, oc]
             remote(blk, blk, agc_s.at[k + d], agc_r.at[k + d], tensor=sib).wait_recv()
 
     def stream():
@@ -355,13 +397,18 @@
         remote(ext.at[pl.ds(256, 16)], ext.at[pl.ds(0, 16)], misc_s.at[2], misc_r.at[2], seq=other)
     )
     dt_raw = lax.dot_general(dt_in[...], stream(), NT, preferred_element_type=F32)
-    dt_raw = dt_raw + dt_bias[...]
+    head_row = lax.broadcasted_iota(jnp.int32, (8, LEN), 0)
+
+    def by_head(ref, heads):
+        values = jnp.zeros(heads.shape, F32)
+        for h in range(8):
+            values = jnp.where(heads == h, ref[h], values)
+        return values
+
+    dt_raw = dt_raw + by_head(dt_bias, head_row)
+    rate = by_head(rate_in, head_row)
     steps[s] = jax.nn.softplus(dt_raw)
     step_send = go(remote(steps.at[s], steps.at[s], misc_s.at[3], misc_r.at[3], seq=other))
-    for i in range(2):
-        cols = slice(i * 256, i * 256 + 256)
-        gate[:, cols] = jnp.dot(stream(), w_zx[:, cols], preferred_element_type=F32).astype(BF16)
-
     n_seg = lengths.shape[0]
     bounds = []
     run = jnp.int32(0)
@@ -379,13 +426,17 @@
 
     def taps_for(i, row):
         if i < 4:
-            return taps_x[row : row + 1, i * 128 : i * 128 + 128]
-        lo = (i - 4) * 64
-        return jnp.concatenate(
-            [t_bc[0, row : row + 1, lo : lo + 64], t_bc[1, row : row + 1, lo : lo + 64]], axis=1
-        )
-
-    for i in range(6):
+            cols = slice(i * 128, i * 128 + 128)
+            return bias_x[:, cols] if row == 4 else conv_x[row : row + 1, cols]
+        k = i - 4
+        if row == 4:
+            pair = [t_bias[e, k : k + 1, :] for e in range(2)]
+        else:
+            pair = [t_conv[e, row, k : k + 1, :] for e in range(2)]
+        return jnp.concatenate(pair, axis=1)
+
+    act_sends = []
+    for i in (4, 0, 1, 2, 3, 5):
         cols = slice(i * 128, i * 128 + 128)
         v = ext[:, cols].astype(F32)
         total = jnp.zeros((LEN, 128), F32) + taps_for(i, 4)
@@ -393,15 +444,12 @@
             lagged = v if j == 0 else pltpu.roll(v, j, 0)
             total = total + taps_for(i, j) * lagged[16:] * masks[j]
         act[s, :, cols] = (total * lax.logistic(total)).astype(BF16)
-    act_send = go(
-        remote(
-            act.at[s, :, pl.ds(0, 640)],
-            act.at[s, :, pl.ds(0, 640)],
-            misc_s.at[4],
-            misc_r.at[4],
-            seq=other,
-        )
-    )
+        if i < 5:
+            tile = act.at[s, :, pl.ds(i * 128, 128)]
+            act_sends.append(go(remote(tile, tile, act_s.at[i], act_r.at[i], seq=other)))
+    for i in range(2):
+        cols = slice(i * 256, i * 256 + 256)
+        gate[:, cols] = jnp.dot(stream(), w_zx[:, cols], preferred_element_type=F32).astype(BF16)
 
     ri = lax.broadcasted_iota(jnp.int32, (LEN, LEN), 0)
     ci = lax.broadcasted_iota(jnp.int32, (LEN, LEN), 1)
@@ -410,7 +458,7 @@
     spread = (head_of == lax.broadcasted_iota(jnp.int32, (8, CHAN), 0)).astype(F32)
 
     def cumulate(dt):
-        return jnp.dot(-rate[...] * dt, upper, precision=HIGH, preferred_element_type=F32)
+        return jnp.dot(-rate * dt, upper, precision=HIGH, preferred_element_type=F32)
 
     def widen(rows):
         return lax.dot_general(rows, spread, TN, precision=HIGH, preferred_element_type=F32)
@@ -437,10 +485,10 @@
         acc[:, cols] = jnp.where(lane < 64, halves[0], halves[1])
 
     step_send.wait_recv()
-    act_send.wait_recv()
+    for sent in act_sends:
+        sent.wait_recv()
     dt_0 = steps[0]
     cum_0 = cumulate(dt_0)
-    end_0 = jnp.sum(-rate[...] * dt_0, axis=1, keepdims=True)
     seg_before = segment_of(bounds, jnp.full((8, LEN), LEN - 1, jnp.int32))
     place = lax.broadcasted_iota(jnp.int32, (8, LEN), 1)
     seg_0 = segment_of(bounds, place)
@@ -456,37 +504,46 @@
     carried = ((seg_own == seg_before) & (s > 0)).astype(F32)
     gain = widen(jnp.exp(cum_r) * carried)
     y_all = acc[:, :CHAN] + jnp.dot(c_own, entry, preferred_element_type=F32) * gain
-    y_all = y_all + skip[...] * act[s, :, :CHAN].astype(F32)
+    y_all = y_all + by_head(skip_in, head_of[:1]) * act[s, :, :CHAN].astype(F32)
     gate_f = gate[...].astype(F32)
     gate[...] = (y_all * (gate_f * lax.logistic(gate_f))).astype(BF16)
     out_load.wait()
 
-    @pl.loop(0, 8)
-    def _(i):
-        cols = pl.ds(pl.multiple_of(i * 512, 512), 512)
-        acc[:, cols] = jnp.dot(gate[...], w_out[:, cols], preferred_element_type=F32)
-
-    def part(d, yy, cc):
-        return pl.ds(pl.multiple_of(((z + d) % 4) * 64 + yy * 32 + cc * 16, 16), 16)
-
-    order = (2, 1, 3, 0)
-    a_copy = {}
-    for d in order:
-        for yy in range(2):
-            send_a[d, yy] = acc[part(d, yy, oc), :].astype(BF16)
-        a_copy[d] = go(
-            remote(send_a.at[d], recv_a.at[d], rsa_s.at[d], rsa_r.at[d], tensor=sib)
+    def part(zz, yy, cc):
+        return pl.ds(pl.multiple_of(zz * 64 + yy * 32 + cc * 16, 16), 16)
+
+    a_copy = []
+    b_copy = []
+
+    def to_pal(q):
+        cols = slice(q * 1024, q * 1024 + 1024)
+        a_copy[q].wait_recv()
+        for zz in range(4):
+            send_b[q, zz] = (
+                acc[part(zz, oy, c), cols] + recv_a[q, zz, oy].astype(F32)
+            ).astype(BF16)
+        b_copy.append(
+            go(remote(send_b.at[q], recv_b.at[q], rsb_s.at[q], rsb_r.at[q], tensor=ypal))
         )
-    b_copy = {}
-    for d in order:
-        a_copy[d].wait_recv()
-        send_b[d] = (acc[part(d, oy, c), :] + recv_a[d, oy].astype(F32)).astype(BF16)
-        b_copy[d] = go(
-            remote(send_b.at[d], recv_b.at[d], rsb_s.at[d], rsb_r.at[d], tensor=ypal)
+        for zz in range(4):
+            keep[q, zz] = acc[part(zz, y, c), cols] + recv_a[q, zz, y].astype(F32)
+
+    for q in range(4):
+        for e in range(2):
+            cols = slice(q * 1024 + e * 512, q * 1024 + e * 512 + 512)
+            acc[:, cols] = jnp.dot(gate[...], w_out[:, cols], preferred_element_type=F32)
+        cols = slice(q * 1024, q * 1024 + 1024)
+        for zz in range(4):
+            for yy in range(2):
+                send_a[q, zz, yy] = acc[part(zz, yy, oc), cols].astype(BF16)
+        a_copy.append(
+            go(remote(send_a.at[q], recv_a.at[q], rsa_s.at[q], rsa_r.at[q], tensor=sib))
         )
-        keep[d] = acc[part(d, y, c), :] + recv_a[d, y].astype(F32)
-
-    def finals_part():
+        if q > 0:
+            to_pal(q - 1)
+    to_pal(3)
+
+    def finals_ready():
         dt_1 = steps[1]
         cum_1 = cumulate(dt_1) + last_0
         ends_0 = jnp.zeros((8, LEN), F32)
@@ -507,33 +564,43 @@
         spot = lax.broadcasted_iota(jnp.int32, (LEN, STATES), 0)
         col_0 = segment_of(bounds, spot)
         col_1 = segment_of(bounds, spot + LEN)
-        for k in range(n_seg):
+
+        def fill(k):
             m_0 = jnp.where(col_0 == k, b_0.astype(F32), 0.0).astype(BF16)
             m_1 = jnp.where(col_1 == k, b_1.astype(F32), 0.0).astype(BF16)
             fin[k] = lax.dot_general(
                 xw_0, m_0, TN, preferred_element_type=F32
             ) + lax.dot_general(xw_1, m_1, TN, preferred_element_type=F32)
 
-    c_copy = {}
-    for d in order:
-        b_copy[d].wait_recv()
-        summed = keep[d] + recv_b[d].astype(F32)
-        if d == 0:
-            keep[0] = summed
-        else:
-            send_c[d] = summed.astype(BF16)
-            c_copy[d] = go(
-                remote(send_c.at[d], recv_c.at[d], rsc_s.at[d], rsc_r.at[d], tensor=zpal[d])
+        return fill
+
+    c_copy = []
+    fill = None
+    for q in range(4):
+        b_copy[q].wait_recv()
+        for d in (2, 1, 3):
+            zz = (z + d) % 4
+            k = q * 4 + d
+            send_c[k] = (keep[q, zz] + recv_b[q, zz].astype(F32)).astype(BF16)
+            c_copy.append(
+                go(remote(send_c.at[k], recv_c.at[k], rsc_s.at[k], rsc_r.at[k], tensor=zpal[d]))
             )
-        if d == 2:
-            finals_part()
-            fin_out = pltpu.make_async_copy(fin, finals, load_sem.at[4])
-            fin_out.start()
-    total = keep[0]
-    for d in (1, 3, 2):
-        c_copy[d].wait_recv()
-        total = total + recv_c[d].astype(F32)
-    mixed[...] = total.astype(BF16)
+        if q == 0:
+            fill = finals_ready()
+        elif q < 3:
+            for k in range(n_seg):
+                if k % 2 == q - 1:
+                    fill(k)
+    fin_out = pltpu.make_async_copy(fin, finals, load_sem.at[4])
+    fin_out.start()
+    for q in range(4):
+        total = keep[q, z] + recv_b[q, z].astype(F32)
+        for i, d in enumerate((2, 1, 3)):
+            c_copy[q * 3 + i].wait_recv()
+            total = total + recv_c[q * 4 + d].astype(F32)
+        mixed[:, q * 1024 : q * 1024 + 1024] = total.astype(BF16)
+    for condition, copy in guarded:
+        pl.when(condition)(copy.wait_send)
     for copy in started:
         copy.wait_send()
     fin_out.wait()
@@ -557,12 +624,9 @@
     n_seg = lengths.shape[0]
     bc_view = proj_bc.transpose(1, 2, 0)
     dt_view = proj_dt.T
-    taps_x = jnp.concatenate([conv_x, bias_x[None], jnp.zeros((3, CHAN), F32)], axis=0)
-    taps_bc = jnp.concatenate(
-        [conv_bc.reshape(4, 128), bias_bc.reshape(1, 128), jnp.zeros((3, 128), F32)], axis=0
-    )
     any_spec = pl.BlockSpec(memory_space=pl.ANY)
     vmem = pl.BlockSpec(memory_space=pltpu.VMEM)
+    smem = pl.BlockSpec(memory_space=pltpu.SMEM)
     dma = pltpu.SemaphoreType.DMA
     mixed, finals = pl.pallas_call(
         layer_kernel,
@@ -570,8 +634,8 @@
             jax.ShapeDtypeStruct((ROWS, WIDE), BF16),
             jax.ShapeDtypeStruct((n_seg, CHAN, STATES), F32),
         ),
-        in_specs=[pl.BlockSpec(memory_space=pltpu.SMEM), any_spec, any_spec, any_spec]
-        + [vmem, vmem, any_spec, vmem, vmem, vmem, any_spec],
+        in_specs=[smem, any_spec, any_spec, any_spec, vmem, vmem, vmem]
+        + [any_spec, any_spec, smem, smem, smem, any_spec],
         out_specs=(vmem, any_spec),
         scratch_shapes=[
             pltpu.VMEM((4, 2, 2, ROWS, WIDE), BF16),
@@ -579,37 +643,24 @@
             pltpu.VMEM((WIDE, 2 * CHAN), BF16),
             pltpu.VMEM((2, 2, 64, WIDE), BF16),
             pltpu.VMEM((CHAN, WIDE), BF16),
-            pltpu.VMEM((2, 8, 128), F32),
+            pltpu.VMEM((2, 4, 2, 64), F32),
+            pltpu.VMEM((2, 2, 64), F32),
             pltpu.VMEM((LEN, CHAN), BF16),
             pltpu.VMEM((16 + LEN, CHAN + 256), BF16),
             pltpu.VMEM((2, LEN, CHAN + 256), BF16),
             pltpu.VMEM((2, 8, LEN), F32),
             pltpu.VMEM((n_seg, CHAN, STATES), F32),
             pltpu.VMEM((LEN, WIDE), F32),
-            pltpu.VMEM((4, ROWS, WIDE), F32),
-            pltpu.VMEM((4, 2, ROWS, WIDE), BF16),
-            pltpu.VMEM((4, 2, ROWS, WIDE), BF16),
-            pltpu.VMEM((4, ROWS, WIDE), BF16),
-            pltpu.VMEM((4, ROWS, WIDE), BF16),
-            pltpu.VMEM((4, ROWS, WIDE), BF16),
-            pltpu.VMEM((4, ROWS, WIDE), BF16),
-            dma((5,)),
-            dma((4,)),
-            dma((4,)),
-            dma((4,)),
-            dma((4,)),
-            dma((4,)),
-            dma((8,)),
-            dma((8,)),
-            dma((5,)),
-            dma((5,)),
-            dma((4,)),
-            dma((4,)),
-            dma((4,)),
-            dma((4,)),
-            dma((4,)),
-            dma((4,)),
-        ],
+            pltpu.VMEM((4, 4, ROWS, WIDE // 4), F32),
+            pltpu.VMEM((4, 4, 2, ROWS, WIDE // 4), BF16),
+            pltpu.VMEM((4, 4, 2, ROWS, WIDE // 4), BF16),
+            pltpu.VMEM((4, 4, ROWS, WIDE // 4), BF16),
+            pltpu.VMEM((4, 4, ROWS, WIDE // 4), BF16),
+            pltpu.VMEM((16, ROWS, WIDE // 4), BF16),
+            pltpu.VMEM((16, ROWS, WIDE // 4), BF16),
+        ]
+        + [dma((k,)) for k in (6, 4, 4, 4, 4, 4, 4, 4, 8, 8, 6, 6, 5, 5)]
+        + [dma((k,)) for k in (4, 4, 4, 4, 16, 16)],
         compiler_params=pltpu.CompilerParams(
             collective_id=0, has_side_effects=True, vmem_limit_bytes=60 << 20
         ),
@@ -619,11 +670,13 @@
         proj_zx,
         bc_view,
         dt_view,
-        taps_x,
-        taps_bc,
-        dt_bias.reshape(8, 1),
-        decay_rate.reshape(8, 1),
-        jnp.repeat(skip_gain, 64).reshape(1, CHAN),
+        conv_x,
+        bias_x.reshape(1, CHAN),
+        conv_bc,
+        bias_bc,
+        dt_bias,
+        decay_rate,
+        skip_gain,
         proj_out,
     )
     return (mixed, finals.reshape(n_seg, 8, 64, STATES))

time: 76.7 us -> 65.4 us (0.85)
  local copies, waits for them, and re-layouts: 9.91 us -> 4.29 us
  Pallas kernels: 63.8 us -> 60.2 us
  other arithmetic: 2.05 us -> 0 us
    reshape x4 -> x0, local copies, waits for them, and re-layouts: 4.16 us -> none  [the longest x1 1.32 us: fused_body(): decay_rate.reshape(8, 1)]
    pallas_call x1, Pallas kernels: 63.8 us -> 60.2 us  [fused_body(): pl.pallas_call(layer_kernel, out_shape=(jax.ShapeDtypeStruct((ROWS, WIDE)...]
    concatenate x2 -> x0, other arithmetic: 2.05 us -> none  [the longest x1 1.39 us: fused_body(): jnp.concatenate([conv_x, bias_x[None], jnp.zeros((3, CHAN), F32)], axis=0)]
where the time goes in v2:
time: 65.4 us; the launch traced here: 65.1 us
  Pallas kernels  60.2 us (92%)
  local copies, waits for them, and re-layouts  4.29 us (7%)
    pallas_call x1, Pallas kernels, fused_body(): pl.pallas_call(layer_kernel, out_shape=(jax.ShapeDtypeStruct((ROWS, WIDE)...  60.2 us
    unnamed x2, local copies, waits for them, and re-layouts  4.29 us

profile of v2, /device:TPU:0, one launch (start us, length us, event | category | flops | bytes accessed | tf_op | source)
XLA Modules:
  0.0 65.1 jit_solution(6917232214268425390)
XLA Ops:
  0.6 60.2 %shard_map.140 = (bf16[16,4096]{1,0:T(8,128)(2,1)}, f32[6,512,128]{2,1,0:T(8,128)}) custom-call(s32[6]{0:T(128)} %lengths.1, bf16[16,4096]{1,0:T(8,128)(2,1)} %tok_in.1, bf16[4096,2,512]{2,1,0:T(2,128)(2,1)} %zx_in.1, bf16[2,64,4096]{2,1,0:T(8,128)(2,1)} %bitcast.5, bf16[8,4096]{1,0:T(8,128)(2,1)} %bitcast.6, f32[4,512]{1,0:T(4,128)} %conv_x.1, ...), custom_call_target="tpu_custom_call" | custom-call | tf_op jit(solution)/shard_map/pallas_call | solution.py:631
  60.9 1.6 %copy.17 = bf16[16,4096]{1,0:T(8,128)(2,1)} copy(bf16[16,4096]{1,0:T(8,128)(2,1)} %get-tuple-element.8) | data formatting | bytes 262144
  62.4 2.7 %copy.18 = f32[6,8,64,128]{3,2,1,0:T(8,128)} copy(f32[6,8,64,128]{3,2,1,0:T(8,128)} %bitcast.4) | data formatting | bytes 3145728
